TPU v7x, 32 devices: a whole 2x2x4 slice. The times are simulated.
32 devices in a mesh: rep: 2 (over x), ctx: 8 (over z, y), tp: 2 (over core).
Axes of the slice: x: 2, y: 2, z: 4, core: 2. Of those that a mesh axis runs over, the one named last changes fastest.
Arguments:
- queries: bfloat16 [4096, 4096], P(('rep', 'ctx'), 'tp'), parts along dimension 0, may hold values from -8 to 8
- rotated_key_rows: bfloat16 [4096, 512], P(('rep', 'ctx'), 'tp'), parts along dimension 0, may hold values from -8 to 8
- ordered_value_rows: bfloat16 [4096, 512], P(('rep', 'ctx'), 'tp'), parts along dimension 0, may hold values from -6 to 6
- block_order: int32 [32], P('rep'), parts along dimension 0, may hold values from 0 to 15, each once
- live_blocks: int32 [32, 12], P('rep'), parts along dimension 0, may hold values from -1 to 15, as said below
Outputs:
- attended: bfloat16 [4096, 4096], P(('rep', 'ctx', 'tp')), parts along dimension 0
- log_norm: float32 [64, 2048], P(('rep', 'tp'), 'ctx'), parts along dimension 0
There are 2 independent parts, one for each index of `rep`. A program takes and returns all parts, laid end to end along the dimension named above; each array names one. Nothing has to cross between parts.
Inputs may be any that keep to these rules, and one draw needn't show every extreme that they name: `live_blocks`: row s names block s in its first slot, then distinct blocks before s, then -1 in every unused slot; row 15 fills all 12 slots.
All inputs are finite; a program needn't handle non-finite values.
Results may differ from a plain program's by a relative error of at most 0.008.
Values may be sent and summed in bfloat16 or wider, within the bound.
A program may use at most 128 MiB of HBM per device.

v0:
```python
import jax
import jax.numpy as jnp
from jax import lax
from jax.sharding import PartitionSpec as P

HEAD_SIZE = 128
BLOCK_TOKENS = 128
NEG_LARGE = -1e30


def body(queries, rotated_key_rows, ordered_value_rows, block_order, live_blocks):
    tok_rows = queries.shape[0]
    kv_local = rotated_key_rows.shape[1] // HEAD_SIZE
    heads_local = queries.shape[1] // HEAD_SIZE
    query_groups = heads_local // kv_local
    blocks_total = block_order.shape[0]
    blocks_here = tok_rows // BLOCK_TOKENS
    factor = HEAD_SIZE ** (-0.5)
    shard_index = lax.axis_index("ctx")
    block_ids = jnp.arange(blocks_total, dtype=jnp.int32)
    my_blocks = lax.dynamic_slice_in_dim(block_order, shard_index * blocks_here, blocks_here)
    my_lists = jnp.take(live_blocks, my_blocks, axis=0)
    live_table = jnp.any(my_lists[:, :, None] == block_ids[None, None, :], axis=1)
    within = jnp.arange(BLOCK_TOKENS, dtype=jnp.int32)
    causal_square = within[None, :] <= within[:, None]
    query_heads = queries.reshape(tok_rows, kv_local, query_groups, HEAD_SIZE)
    carried = tuple(
        (
            (
                jnp.full((kv_local, query_groups, BLOCK_TOKENS), NEG_LARGE, jnp.float32),
                jnp.zeros((kv_local, query_groups, BLOCK_TOKENS), jnp.float32),
                jnp.zeros((kv_local, query_groups, BLOCK_TOKENS, HEAD_SIZE), jnp.float32),
            )
            for block_local in range(blocks_here)
        )
    )
    key_piece = lax.all_gather(rotated_key_rows, "ctx", axis=0, tiled=True)
    value_piece = lax.all_gather(ordered_value_rows, "ctx", axis=0, tiled=True)
    key_blocks = key_piece.shape[0] // BLOCK_TOKENS

    def one_key_block(turn_index, states):
        offset = turn_index * BLOCK_TOKENS
        key_part = lax.dynamic_slice_in_dim(key_piece, offset, BLOCK_TOKENS).reshape(
            BLOCK_TOKENS, kv_local, HEAD_SIZE
        )
        value_part = lax.dynamic_slice_in_dim(value_piece, offset, BLOCK_TOKENS).reshape(
            BLOCK_TOKENS, kv_local, HEAD_SIZE
        )
        key_seq = block_order[offset // BLOCK_TOKENS]
        updated = []
        for block_local in range(blocks_here):
            query_part = query_heads[block_local * BLOCK_TOKENS : (block_local + 1) * BLOCK_TOKENS]
            allowed = (key_seq != my_blocks[block_local]) | causal_square

            def compute_tile(current):
                running, denominator, weighted = current
                scores = (
                    jnp.einsum(
                        "qhgd,khd->hgqk", query_part, key_part, preferred_element_type=jnp.float32
                    )
                    * factor
                )
                scores = jnp.where(allowed, scores, NEG_LARGE)
                new_peak = jnp.maximum(running, jnp.max(scores, axis=-1))
                weights = jnp.where(allowed, jnp.exp(scores - new_peak[..., None]), 0.0)
                rescale = jnp.exp(running - new_peak)
                denominator = denominator * rescale + jnp.sum(weights, axis=-1)
                weighted = weighted * rescale[..., None] + jnp.einsum(
                    "hgqk,khd->hgqd",
                    weights.astype(jnp.bfloat16),
                    value_part,
                    preferred_element_type=jnp.float32,
                )
                return (new_peak, denominator, weighted)

            updated.append(
                lax.cond(
                    live_table[block_local, key_seq],
                    compute_tile,
                    lambda current: current,
                    states[block_local],
                )
            )
        return tuple(updated)

    states = lax.fori_loop(0, key_blocks, one_key_block, carried)
    running = jnp.concatenate([item[0] for item in states], axis=2)
    denominator = jnp.concatenate([item[1] for item in states], axis=2)
    weighted = jnp.concatenate([item[2] for item in states], axis=2)
    normed = weighted / denominator[..., None]
    merged_out = (
        jnp.transpose(normed, (2, 0, 1, 3))
        .reshape(tok_rows, heads_local * HEAD_SIZE)
        .astype(jnp.bfloat16)
    )
    log_norm = (running + jnp.log(denominator)).reshape(heads_local, tok_rows)
    attended = lax.all_to_all(merged_out, "tp", split_axis=0, concat_axis=1, tiled=True)
    return (attended, log_norm)


def solution(mesh):
    placed = (
        P(("rep", "ctx"), "tp"),
        P(("rep", "ctx"), "tp"),
        P(("rep", "ctx"), "tp"),
        P("rep"),
        P("rep", None),
    )
    return jax.shard_map(
        body,
        mesh=mesh,
        in_specs=placed,
        out_specs=(P(("rep", "ctx", "tp"), None), P(("rep", "tp"), "ctx")),
        check_vma=False,
    )
```

profile of v0, /device:TPU:0, one launch (start us, length us, event | category | flops | bytes accessed | tf_op | source)
XLA Modules:
  0.0 250.6 jit_solution(15988656583783142846)
XLA Ops:
  13.7 39.1 %all-gather.3.cloned.1.call-done = bf16[2048,256]{0,1:T(8,128)(2,1)} async-done(((bf16[256,256]{0,1:T(8,128)(2,1)}), bf16[2048,256]{0,1:T(8,128)(2,1)}) %all-gather.3.cloned.1.call-update) | async-done | bytes 1048592 | tf_op jit(solution)/shard_map/all_gather | solution.py:37
  52.8 40.5 %all-gather.5.cloned.1.call-done = bf16[2048,256]{0,1:T(8,128)(2,1)} async-done(((bf16[256,256]{0,1:T(8,128)(2,1)}), bf16[2048,256]{0,1:T(8,128)(2,1)}) %all-gather.5.cloned.1.call-update) | async-done | bytes 1048592 | tf_op jit(solution)/shard_map/all_gather | solution.py:38
  93.5 141.2 %while.27 = (s32[]{:T(128)}, f32[2,8,128]{2,1,0:T(8,128)S(1)}, f32[2,8,128]{2,1,0:T(8,128)S(1)}, f32[2,8,128,128]{3,2,1,0:T(8,128)S(1)}, f32[2,8,128]{2,1,0:T(8,...) while((s32[]{:T(128)}, f32[2,8,128]{2,1,0:T(8,128)S(1)}, ...), condition=%wide.region_10.11_spmd.clone.clone, body=%wide.region_1.10_spmd.clone.clone.sunk | while | flops 274260000 | bytes 12501754 | solution.py:86
  98.9 2.0 conditional.8
  106.3 3.3 %conditional.9 = ((f32[2,8,128]{2,1,0:T(8,128)S(1)}, f32[2,8,128]{2,1,0:T(8,128)S(1)}, f32[2,8,128,128]{3,2,1,0:T(8,128)S(1)})) conditional(s32[]{:T(128)} %bitcast.60, (f32[2,8,128]{2,1,0:T(8,128)S(1)}, f32[2,8,128]{2,1,0:T(8,128)S(1)}, f32[2,8,128,128]{3,2,1,0:T(8,128)S(1)}) %tuple.96, (s32[2]{0:T(128)S(1)}, s32[]{:T(128)}, ...), branch_computations={%region_6.6_spmd, %region_7.9_spmd} | conditional | flops 137121792 | bytes 6111282 | solution.py:77
  115.0 2.0 conditional.8
  117.1 3.3 %conditional.9 = ((f32[2,8,128]{2,1,0:T(8,128)S(1)}, f32[2,8,128]{2,1,0:T(8,128)S(1)}, f32[2,8,128,128]{3,2,1,0:T(8,128)S(1)})) conditional(s32[]{:T(128)} %bitcast.60, (f32[2,8,128]{2,1,0:T(8,128)S(1)}, f32[2,8,128]{2,1,0:T(8,128)S(1)}, f32[2,8,128,128]{3,2,1,0:T(8,128)S(1)}) %tuple.96, (s32[2]{0:T(128)S(1)}, s32[]{:T(128)}, ...), branch_computations={%region_6.6_spmd, %region_7.9_spmd} | conditional | flops 137121792 | bytes 6111282 | solution.py:77
  125.8 2.0 conditional.8
  127.8 3.3 %conditional.9 = ((f32[2,8,128]{2,1,0:T(8,128)S(1)}, f32[2,8,128]{2,1,0:T(8,128)S(1)}, f32[2,8,128,128]{3,2,1,0:T(8,128)S(1)})) conditional(s32[]{:T(128)} %bitcast.60, (f32[2,8,128]{2,1,0:T(8,128)S(1)}, f32[2,8,128]{2,1,0:T(8,128)S(1)}, f32[2,8,128,128]{3,2,1,0:T(8,128)S(1)}) %tuple.96, (s32[2]{0:T(128)S(1)}, s32[]{:T(128)}, ...), branch_computations={%region_6.6_spmd, %region_7.9_spmd} | conditional | flops 137121792 | bytes 6111282 | solution.py:77
  136.5 2.0 conditional.8
  138.5 3.3 %conditional.9 = ((f32[2,8,128]{2,1,0:T(8,128)S(1)}, f32[2,8,128]{2,1,0:T(8,128)S(1)}, f32[2,8,128,128]{3,2,1,0:T(8,128)S(1)})) conditional(s32[]{:T(128)} %bitcast.60, (f32[2,8,128]{2,1,0:T(8,128)S(1)}, f32[2,8,128]{2,1,0:T(8,128)S(1)}, f32[2,8,128,128]{3,2,1,0:T(8,128)S(1)}) %tuple.96, (s32[2]{0:T(128)S(1)}, s32[]{:T(128)}, ...), branch_computations={%region_6.6_spmd, %region_7.9_spmd} | conditional | flops 137121792 | bytes 6111282 | solution.py:77
  147.2 2.0 conditional.8
  149.2 3.3 %conditional.9 = ((f32[2,8,128]{2,1,0:T(8,128)S(1)}, f32[2,8,128]{2,1,0:T(8,128)S(1)}, f32[2,8,128,128]{3,2,1,0:T(8,128)S(1)})) conditional(s32[]{:T(128)} %bitcast.60, (f32[2,8,128]{2,1,0:T(8,128)S(1)}, f32[2,8,128]{2,1,0:T(8,128)S(1)}, f32[2,8,128,128]{3,2,1,0:T(8,128)S(1)}) %tuple.96, (s32[2]{0:T(128)S(1)}, s32[]{:T(128)}, ...), branch_computations={%region_6.6_spmd, %region_7.9_spmd} | conditional | flops 137121792 | bytes 6111282 | solution.py:77
  163.4 3.3 %conditional.9 = ((f32[2,8,128]{2,1,0:T(8,128)S(1)}, f32[2,8,128]{2,1,0:T(8,128)S(1)}, f32[2,8,128,128]{3,2,1,0:T(8,128)S(1)})) conditional(s32[]{:T(128)} %bitcast.60, (f32[2,8,128]{2,1,0:T(8,128)S(1)}, f32[2,8,128]{2,1,0:T(8,128)S(1)}, f32[2,8,128,128]{3,2,1,0:T(8,128)S(1)}) %tuple.96, (s32[2]{0:T(128)S(1)}, s32[]{:T(128)}, ...), branch_computations={%region_6.6_spmd, %region_7.9_spmd} | conditional | flops 137121792 | bytes 6111282 | solution.py:77
  172.1 3.3 %conditional.9 = ((f32[2,8,128]{2,1,0:T(8,128)S(1)}, f32[2,8,128]{2,1,0:T(8,128)S(1)}, f32[2,8,128,128]{3,2,1,0:T(8,128)S(1)})) conditional(s32[]{:T(128)} %bitcast.60, (f32[2,8,128]{2,1,0:T(8,128)S(1)}, f32[2,8,128]{2,1,0:T(8,128)S(1)}, f32[2,8,128,128]{3,2,1,0:T(8,128)S(1)}) %tuple.96, (s32[2]{0:T(128)S(1)}, s32[]{:T(128)}, ...), branch_computations={%region_6.6_spmd, %region_7.9_spmd} | conditional | flops 137121792 | bytes 6111282 | solution.py:77
  180.8 2.0 conditional.8
  182.8 3.3 %conditional.9 = ((f32[2,8,128]{2,1,0:T(8,128)S(1)}, f32[2,8,128]{2,1,0:T(8,128)S(1)}, f32[2,8,128,128]{3,2,1,0:T(8,128)S(1)})) conditional(s32[]{:T(128)} %bitcast.60, (f32[2,8,128]{2,1,0:T(8,128)S(1)}, f32[2,8,128]{2,1,0:T(8,128)S(1)}, f32[2,8,128,128]{3,2,1,0:T(8,128)S(1)}) %tuple.96, (s32[2]{0:T(128)S(1)}, s32[]{:T(128)}, ...), branch_computations={%region_6.6_spmd, %region_7.9_spmd} | conditional | flops 137121792 | bytes 6111282 | solution.py:77
  191.5 2.0 conditional.8
  193.5 3.3 %conditional.9 = ((f32[2,8,128]{2,1,0:T(8,128)S(1)}, f32[2,8,128]{2,1,0:T(8,128)S(1)}, f32[2,8,128,128]{3,2,1,0:T(8,128)S(1)})) conditional(s32[]{:T(128)} %bitcast.60, (f32[2,8,128]{2,1,0:T(8,128)S(1)}, f32[2,8,128]{2,1,0:T(8,128)S(1)}, f32[2,8,128,128]{3,2,1,0:T(8,128)S(1)}) %tuple.96, (s32[2]{0:T(128)S(1)}, s32[]{:T(128)}, ...), branch_computations={%region_6.6_spmd, %region_7.9_spmd} | conditional | flops 137121792 | bytes 6111282 | solution.py:77
  207.7 3.3 %conditional.9 = ((f32[2,8,128]{2,1,0:T(8,128)S(1)}, f32[2,8,128]{2,1,0:T(8,128)S(1)}, f32[2,8,128,128]{3,2,1,0:T(8,128)S(1)})) conditional(s32[]{:T(128)} %bitcast.60, (f32[2,8,128]{2,1,0:T(8,128)S(1)}, f32[2,8,128]{2,1,0:T(8,128)S(1)}, f32[2,8,128,128]{3,2,1,0:T(8,128)S(1)}) %tuple.96, (s32[2]{0:T(128)S(1)}, s32[]{:T(128)}, ...), branch_computations={%region_6.6_spmd, %region_7.9_spmd} | conditional | flops 137121792 | bytes 6111282 | solution.py:77
  221.9 2.0 conditional.8
  229.4 2.0 conditional.8
  231.4 3.3 %conditional.9 = ((f32[2,8,128]{2,1,0:T(8,128)S(1)}, f32[2,8,128]{2,1,0:T(8,128)S(1)}, f32[2,8,128,128]{3,2,1,0:T(8,128)S(1)})) conditional(s32[]{:T(128)} %bitcast.60, (f32[2,8,128]{2,1,0:T(8,128)S(1)}, f32[2,8,128]{2,1,0:T(8,128)S(1)}, f32[2,8,128,128]{3,2,1,0:T(8,128)S(1)}) %tuple.96, (s32[2]{0:T(128)S(1)}, s32[]{:T(128)}, ...), branch_computations={%region_6.6_spmd, %region_7.9_spmd} | conditional | flops 137121792 | bytes 6111282 | solution.py:77
  236.6 4.6 %all_to_all.16 = bf16[2,128,2048]{2,1,0:T(8,128)(2,1)S(1)} all-to-all(bf16[2,128,2048]{2,1,0:T(8,128)(2,1)S(1)} %convert_element_type.44), channel_id=1, replica_groups=mesh['rep'=2,'ctx'=8,'tp'=2] {'tp'}, dimensions={0} | all-to-all | bytes 2097152 | tf_op jit(solution)/shard_map/all_to_all | solution.py:97
  (258 shorter events, 78.4 us)
Async XLA Ops:
  7.2 5.8 %copy-start = (s32[16,12]{1,0:T(8,128)S(1)}, s32[16,12]{1,0:T(8,128)}, u32[]{:S(2)}) copy-start(s32[16,12]{1,0:T(8,128)} %param.15) | copy-start | bytes 2308
  7.2 45.6 %all-gather.3.cloned.1.call-start = ((), (), s32[]{:S(2)}) async-start(), calls=%async_computation.1 | async-start | bytes 1179648 | tf_op jit(solution)/shard_map/all_gather | solution.py:37
  8.9 84.3 %all-gather.5.cloned.1.call-start = ((), (), s32[]{:S(2)}) async-start(), calls=%async_computation.2 | async-start | bytes 1179648 | tf_op jit(solution)/shard_map/all_gather | solution.py:38
  12.1 0.7 copy-start.1
Sparse Core Ops, SparseCore 0:
  10.6 42.1 all-gather.2
  54.8 38.3 all-gather.4
where the time goes:
time: 253 us; the launch traced here: 251 us
  waiting for transfers between devices  79.6 us (31%)
  loops' own time  74.1 us (29%)
  local copies, waits for them, and re-layouts  50.8 us (20%)
  matrix products  21 us (8%)
  between operations  14.2 us (6%)
  other arithmetic  6.35 us (3%)
  blocking collectives  4.58 us (2%)
    another operation x1, loops' own time, body(): states = lax.fori_loop(0, key_blocks, one_key_block, carried)  52.4 us
    all_gather x1, waiting for transfers between devices, body(): value_piece = lax.all_gather(ordered_value_rows, 'ctx', axis=0, tiled=True)  40.5 us
    all_gather x1, waiting for transfers between devices, body(): key_piece = lax.all_gather(rotated_key_rows, 'ctx', axis=0, tiled=True)  39.1 us
    another operation x32, loops' own time, one_key_block(): lax.cond(live_table[block_local, key_seq], compute_tile, lambda current:...  21.7 us
    dynamic_slice x16, local copies, waits for them, and re-layouts, one_key_block(): lax.dynamic_slice_in_dim(value_piece, offset, BLOCK_TOKENS)  14.3 us
    dot_general x20, matrix products, compute_tile(): jnp.einsum('hgqk,khd->hgqd', weights.astype(jnp.bfloat16), value_part, pr...  13.7 us
    dynamic_slice x16, local copies, waits for them, and re-layouts, one_key_block(): live_table[block_local, key_seq]  10.6 us
    dynamic_slice x16, local copies, waits for them, and re-layouts, one_key_block(): key_seq = block_order[offset // BLOCK_TOKENS]  9.39 us
  transfers between devices with their start and end apart: 2, of which 2 were waited for; matrix products, arithmetic and copies ran while one was open for 2% of the time, Pallas kernels for 0%

commit v1 on v0

--- a/solution.py
+++ b/solution.py
@@ -6,6 +6,27 @@
 HEAD_SIZE = 128
 BLOCK_TOKENS = 128
 NEG_LARGE = -1e30
+
+
+def in_order(blocks, dim):
+    blocks = jnp.moveaxis(blocks, 0, dim)
+    shape = blocks.shape
+    return blocks.reshape(*shape[:dim], shape[dim] * shape[dim + 1], *shape[dim + 2 :])
+
+
+def grow_blocks(x, axis):
+    peers, index = (lax.axis_size(axis), lax.axis_index(axis))
+    tiles, apart = (x[None], 1)
+    while apart < peers:
+        other = lax.ppermute(tiles, axis, [(i, i ^ apart) for i in range(peers)])
+        low = index & apart == 0
+        tiles = jnp.concatenate([jnp.where(low, tiles, other), jnp.where(low, other, tiles)])
+        apart *= 2
+    return tiles
+
+
+def gather_by_bits(shard, axis, dim):
+    return in_order(grow_blocks(shard, axis), dim)
 
 
 def body(queries, rotated_key_rows, ordered_value_rows, block_order, live_blocks):
@@ -34,7 +55,7 @@
             for block_local in range(blocks_here)
         )
     )
-    key_piece = lax.all_gather(rotated_key_rows, "ctx", axis=0, tiled=True)
+    key_piece = gather_by_bits(rotated_key_rows, "ctx", 0)
     value_piece = lax.all_gather(ordered_value_rows, "ctx", axis=0, tiled=True)
     key_blocks = key_piece.shape[0] // BLOCK_TOKENS
 

time: 253 us -> 235 us (0.929)
  waiting for transfers between devices: 79.6 us -> 41.6 us
  local copies, waits for them, and re-layouts: 50.8 us -> 63.4 us
  starting transfers between devices: 0.08 us -> 7.49 us
  loops' own time: 74.1 us -> 70.6 us
  other arithmetic: 6.35 us -> 9.31 us
    all_gather x1 -> x0, waiting for transfers between devices: 39.1 us -> none  [body(): key_piece = lax.all_gather(rotated_key_rows, 'ctx', axis=0, tiled=True)]
    ppermute x0 -> x3, waiting for transfers between devices: none -> 30.1 us  [grow_blocks(): other = lax.ppermute(tiles, axis, [(i, i ^ apart) for i in range(peers)])]
    all_gather x1, waiting for transfers between devices: 40.5 us -> 11.5 us  [body(): value_piece = lax.all_gather(ordered_value_rows, 'ctx', axis=0, tiled=True)]
    dynamic_slice x0 -> x32, local copies, waits for them, and re-layouts: none -> 15.3 us  [one_key_block(): lax.dynamic_slice_in_dim(key_piece, offset, BLOCK_TOKENS)]
    ppermute x0 -> x3, starting transfers between devices: none -> 7.45 us  [grow_blocks(): other = lax.ppermute(tiles, axis, [(i, i ^ apart) for i in range(peers)])]
    unnamed x9 -> x8, local copies, waits for them, and re-layouts: 6.79 us -> 5.13 us
  transfers between devices with their start and end apart: 2 -> 4, of which waited for: 2 -> 4; matrix products, arithmetic and copies ran while one was open for 2% -> 3% of each run, Pallas kernels for 0% -> 0%
where the time goes in v1:
time: 235 us; the launch traced here: 232 us
  loops' own time  70.6 us (30%)
  local copies, waits for them, and re-layouts  63.4 us (27%)
  waiting for transfers between devices  41.6 us (18%)
  matrix products  21 us (9%)
  between operations  14.2 us (6%)
  other arithmetic  9.31 us (4%)
  starting transfers between devices  7.49 us (3%)
  blocking collectives  4.58 us (2%)
    another operation x1, loops' own time, body(): states = lax.fori_loop(0, key_blocks, one_key_block, carried)  50.5 us
    ppermute x3, waiting for transfers between devices, grow_blocks(): other = lax.ppermute(tiles, axis, [(i, i ^ apart) for i in range(peers)])  30.1 us
    another operation x32, loops' own time, one_key_block(): lax.cond(live_table[block_local, key_seq], compute_tile, lambda current:...  20.1 us
    dynamic_slice x32, local copies, waits for them, and re-layouts, one_key_block(): lax.dynamic_slice_in_dim(key_piece, offset, BLOCK_TOKENS)  15.3 us
    dot_general x20, matrix products, compute_tile(): jnp.einsum('hgqk,khd->hgqd', weights.astype(jnp.bfloat16), value_part, pr...  13.7 us
    dynamic_slice x16, local copies, waits for them, and re-layouts, one_key_block(): lax.dynamic_slice_in_dim(value_piece, offset, BLOCK_TOKENS)  13.6 us
    all_gather x1, waiting for transfers between devices, body(): value_piece = lax.all_gather(ordered_value_rows, 'ctx', axis=0, tiled=True)  11.5 us
    dynamic_slice x16, local copies, waits for them, and re-layouts, one_key_block(): live_table[block_local, key_seq]  10.6 us
  transfers between devices with their start and end apart: 4, of which 4 were waited for; matrix products, arithmetic and copies ran while one was open for 3% of the time, Pallas kernels for 0%

profile of v1, /device:TPU:0, one launch (start us, length us, event | category | flops | bytes accessed | tf_op | source)
XLA Modules:
  0.0 232.1 jit_solution(7165075657095704665)
XLA Ops:
  7.2 3.1 %collective-permute-start = (bf16[1,256,256]{2,1,0:T(8,128)(2,1)}, bf16[1,256,256]{2,1,0:T(8,128)(2,1)S(1)}, u32[]{:S(2)}, u32[]{:S(2)}) collective-permute-start(bf16[1,256,256]{2,1,0:T(8,128)(2,1)} %bitcast.77), channel_id=1, source_target_pairs={{0,2},{2,0},{4,6},{6,4},{8,10},{10,8},{12,14},{14,12},{1,3},{3,1},... | collective-permute-start | bytes 393224 | tf_op jit(solution)/shard_map/ppermute | solution.py:21
  12.0 2.0 collective-permute-done
  16.9 5.6 %collective-permute-done.1 = bf16[2,256,256]{2,1,0:T(8,128)(2,1)S(1)} collective-permute-done((bf16[2,256,256]{2,1,0:T(8,128)(2,1)S(1)}, bf16[2,256,256]{2,1,0:T(8,128)(2,1)S(1)}, u32[]{:S(2)}, u32[]{:S(2)}) %collective-permute-start.1) | collective-permute-done | bytes 262176 | tf_op jit(solution)/shard_map/ppermute | solution.py:21
  23.4 2.5 %collective-permute-start.2 = (bf16[4,256,256]{2,1,0:T(8,128)(2,1)}, bf16[4,256,256]{2,1,0:T(8,128)(2,1)S(1)}, u32[]{:S(2)}, u32[]{:S(2)}) collective-permute-start(bf16[4,256,256]{2,1,0:T(8,128)(2,1)} %pad_maximum_fusion.1), channel_id=1, source_target_pairs={{0,8},{2,10},{4,12},{6,14},{8,0},{10,2},{12,4},{14,6},{1,9},{3,11}... | collective-permute-start | bytes 1572872 | tf_op jit(solution)/shard_map/ppermute | solution.py:21
  28.8 22.5 %collective-permute-done.2 = bf16[4,256,256]{2,1,0:T(8,128)(2,1)S(1)} collective-permute-done((bf16[4,256,256]{2,1,0:T(8,128)(2,1)}, bf16[4,256,256]{2,1,0:T(8,128)(2,1)S(1)}, u32[]{:S(2)}, u32[]{:S(2)}) %collective-permute-start.2) | collective-permute-done | bytes 524320 | tf_op jit(solution)/shard_map/ppermute | solution.py:21
  52.4 11.5 %all-gather.2.cloned.1.call-done = bf16[2048,256]{0,1:T(8,128)(2,1)} async-done(((bf16[256,256]{0,1:T(8,128)(2,1)}), bf16[2048,256]{0,1:T(8,128)(2,1)}) %all-gather.2.cloned.1.call-update) | async-done | bytes 1048592 | tf_op jit(solution)/shard_map/all_gather | solution.py:59
  64.1 152.1 %while.27 = (s32[]{:T(128)}, f32[2,8,128]{2,1,0:T(8,128)S(1)}, f32[2,8,128]{2,1,0:T(8,128)S(1)}, f32[2,8,128,128]{3,2,1,0:T(8,128)S(1)}, f32[2,8,128]{2,1,0:T(8,...) while((s32[]{:T(128)}, f32[2,8,128]{2,1,0:T(8,128)S(1)}, ...), condition=%wide.region_10.11_spmd.clone.clone, body=%wide.region_1.10_spmd.clone.clone.sunk | while | flops 274260000 | bytes 12632830 | solution.py:107
  70.4 2.0 conditional.8
  78.6 3.1 %conditional.9 = ((f32[2,8,128]{2,1,0:T(8,128)S(1)}, f32[2,8,128]{2,1,0:T(8,128)S(1)}, f32[2,8,128,128]{3,2,1,0:T(8,128)S(1)})) conditional(s32[]{:T(128)} %bitcast.64, (f32[2,8,128]{2,1,0:T(8,128)S(1)}, f32[2,8,128]{2,1,0:T(8,128)S(1)}, f32[2,8,128,128]{3,2,1,0:T(8,128)S(1)}) %tuple.96, (s32[2]{0:T(128)S(1)}, s32[]{:T(128)}, ...), branch_computations={%region_6.6_spmd, %region_7.9_spmd} | conditional | flops 137121792 | bytes 6111282 | solution.py:98
  88.0 2.0 conditional.8
  89.9 3.1 %conditional.9 = ((f32[2,8,128]{2,1,0:T(8,128)S(1)}, f32[2,8,128]{2,1,0:T(8,128)S(1)}, f32[2,8,128,128]{3,2,1,0:T(8,128)S(1)})) conditional(s32[]{:T(128)} %bitcast.64, (f32[2,8,128]{2,1,0:T(8,128)S(1)}, f32[2,8,128]{2,1,0:T(8,128)S(1)}, f32[2,8,128,128]{3,2,1,0:T(8,128)S(1)}) %tuple.96, (s32[2]{0:T(128)S(1)}, s32[]{:T(128)}, ...), branch_computations={%region_6.6_spmd, %region_7.9_spmd} | conditional | flops 137121792 | bytes 6111282 | solution.py:98
  101.2 3.1 %conditional.9 = ((f32[2,8,128]{2,1,0:T(8,128)S(1)}, f32[2,8,128]{2,1,0:T(8,128)S(1)}, f32[2,8,128,128]{3,2,1,0:T(8,128)S(1)})) conditional(s32[]{:T(128)} %bitcast.64, (f32[2,8,128]{2,1,0:T(8,128)S(1)}, f32[2,8,128]{2,1,0:T(8,128)S(1)}, f32[2,8,128,128]{3,2,1,0:T(8,128)S(1)}) %tuple.96, (s32[2]{0:T(128)S(1)}, s32[]{:T(128)}, ...), branch_computations={%region_6.6_spmd, %region_7.9_spmd} | conditional | flops 137121792 | bytes 6111282 | solution.py:98
  110.6 2.0 conditional.8
  112.5 3.1 %conditional.9 = ((f32[2,8,128]{2,1,0:T(8,128)S(1)}, f32[2,8,128]{2,1,0:T(8,128)S(1)}, f32[2,8,128,128]{3,2,1,0:T(8,128)S(1)})) conditional(s32[]{:T(128)} %bitcast.64, (f32[2,8,128]{2,1,0:T(8,128)S(1)}, f32[2,8,128]{2,1,0:T(8,128)S(1)}, f32[2,8,128,128]{3,2,1,0:T(8,128)S(1)}) %tuple.96, (s32[2]{0:T(128)S(1)}, s32[]{:T(128)}, ...), branch_computations={%region_6.6_spmd, %region_7.9_spmd} | conditional | flops 137121792 | bytes 6111282 | solution.py:98
  121.9 2.0 conditional.8
  123.9 3.1 %conditional.9 = ((f32[2,8,128]{2,1,0:T(8,128)S(1)}, f32[2,8,128]{2,1,0:T(8,128)S(1)}, f32[2,8,128,128]{3,2,1,0:T(8,128)S(1)})) conditional(s32[]{:T(128)} %bitcast.64, (f32[2,8,128]{2,1,0:T(8,128)S(1)}, f32[2,8,128]{2,1,0:T(8,128)S(1)}, f32[2,8,128,128]{3,2,1,0:T(8,128)S(1)}) %tuple.96, (s32[2]{0:T(128)S(1)}, s32[]{:T(128)}, ...), branch_computations={%region_6.6_spmd, %region_7.9_spmd} | conditional | flops 137121792 | bytes 6111282 | solution.py:98
  139.5 3.1 %conditional.9 = ((f32[2,8,128]{2,1,0:T(8,128)S(1)}, f32[2,8,128]{2,1,0:T(8,128)S(1)}, f32[2,8,128,128]{3,2,1,0:T(8,128)S(1)})) conditional(s32[]{:T(128)} %bitcast.64, (f32[2,8,128]{2,1,0:T(8,128)S(1)}, f32[2,8,128]{2,1,0:T(8,128)S(1)}, f32[2,8,128,128]{3,2,1,0:T(8,128)S(1)}) %tuple.96, (s32[2]{0:T(128)S(1)}, s32[]{:T(128)}, ...), branch_computations={%region_6.6_spmd, %region_7.9_spmd} | conditional | flops 137121792 | bytes 6111282 | solution.py:98
  148.9 3.1 %conditional.9 = ((f32[2,8,128]{2,1,0:T(8,128)S(1)}, f32[2,8,128]{2,1,0:T(8,128)S(1)}, f32[2,8,128,128]{3,2,1,0:T(8,128)S(1)})) conditional(s32[]{:T(128)} %bitcast.64, (f32[2,8,128]{2,1,0:T(8,128)S(1)}, f32[2,8,128]{2,1,0:T(8,128)S(1)}, f32[2,8,128,128]{3,2,1,0:T(8,128)S(1)}) %tuple.96, (s32[2]{0:T(128)S(1)}, s32[]{:T(128)}, ...), branch_computations={%region_6.6_spmd, %region_7.9_spmd} | conditional | flops 137121792 | bytes 6111282 | solution.py:98
  160.2 3.1 %conditional.9 = ((f32[2,8,128]{2,1,0:T(8,128)S(1)}, f32[2,8,128]{2,1,0:T(8,128)S(1)}, f32[2,8,128,128]{3,2,1,0:T(8,128)S(1)})) conditional(s32[]{:T(128)} %bitcast.64, (f32[2,8,128]{2,1,0:T(8,128)S(1)}, f32[2,8,128]{2,1,0:T(8,128)S(1)}, f32[2,8,128,128]{3,2,1,0:T(8,128)S(1)}) %tuple.96, (s32[2]{0:T(128)S(1)}, s32[]{:T(128)}, ...), branch_computations={%region_6.6_spmd, %region_7.9_spmd} | conditional | flops 137121792 | bytes 6111282 | solution.py:98
  171.5 3.1 %conditional.9 = ((f32[2,8,128]{2,1,0:T(8,128)S(1)}, f32[2,8,128]{2,1,0:T(8,128)S(1)}, f32[2,8,128,128]{3,2,1,0:T(8,128)S(1)})) conditional(s32[]{:T(128)} %bitcast.64, (f32[2,8,128]{2,1,0:T(8,128)S(1)}, f32[2,8,128]{2,1,0:T(8,128)S(1)}, f32[2,8,128,128]{3,2,1,0:T(8,128)S(1)}) %tuple.96, (s32[2]{0:T(128)S(1)}, s32[]{:T(128)}, ...), branch_computations={%region_6.6_spmd, %region_7.9_spmd} | conditional | flops 137121792 | bytes 6111282 | solution.py:98
  187.2 3.1 %conditional.9 = ((f32[2,8,128]{2,1,0:T(8,128)S(1)}, f32[2,8,128]{2,1,0:T(8,128)S(1)}, f32[2,8,128,128]{3,2,1,0:T(8,128)S(1)})) conditional(s32[]{:T(128)} %bitcast.64, (f32[2,8,128]{2,1,0:T(8,128)S(1)}, f32[2,8,128]{2,1,0:T(8,128)S(1)}, f32[2,8,128,128]{3,2,1,0:T(8,128)S(1)}) %tuple.96, (s32[2]{0:T(128)S(1)}, s32[]{:T(128)}, ...), branch_computations={%region_6.6_spmd, %region_7.9_spmd} | conditional | flops 137121792 | bytes 6111282 | solution.py:98
  211.1 2.0 conditional.8
  213.1 3.1 %conditional.9 = ((f32[2,8,128]{2,1,0:T(8,128)S(1)}, f32[2,8,128]{2,1,0:T(8,128)S(1)}, f32[2,8,128,128]{3,2,1,0:T(8,128)S(1)})) conditional(s32[]{:T(128)} %bitcast.64, (f32[2,8,128]{2,1,0:T(8,128)S(1)}, f32[2,8,128]{2,1,0:T(8,128)S(1)}, f32[2,8,128,128]{3,2,1,0:T(8,128)S(1)}) %tuple.96, (s32[2]{0:T(128)S(1)}, s32[]{:T(128)}, ...), branch_computations={%region_6.6_spmd, %region_7.9_spmd} | conditional | flops 137121792 | bytes 6111282 | solution.py:98
  218.1 4.6 %all_to_all.16 = bf16[2,128,2048]{2,1,0:T(8,128)(2,1)S(1)} all-to-all(bf16[2,128,2048]{2,1,0:T(8,128)(2,1)S(1)} %convert_element_type.44), channel_id=1, replica_groups=mesh['rep'=2,'ctx'=8,'tp'=2] {'tp'}, dimensions={0} | all-to-all | bytes 2097152 | tf_op jit(solution)/shard_map/all_to_all | solution.py:118
  (298 shorter events, 103.7 us)
Async XLA Ops:
  7.2 20.9 %copy-start = (s32[16,12]{1,0:T(8,128)S(1)}, s32[16,12]{1,0:T(8,128)}, u32[]{:S(2)}) copy-start(s32[16,12]{1,0:T(8,128)} %param.15) | copy-start | bytes 2308
  7.2 9.7 %copy-start.1 = (s32[16]{0:T(128)S(1)}, s32[16]{0:T(128)}, u32[]{:S(2)}) copy-start(s32[16]{0:T(128)} %param.14) | copy-start | bytes 196
  7.2 56.7 %all-gather.2.cloned.1.call-start = ((), (), s32[]{:S(2)}) async-start(), calls=%async_computation.1 | async-start | bytes 1179648 | tf_op jit(solution)/shard_map/all_gather | solution.py:59
  7.2 6.8 %collective-permute-start = (bf16[1,256,256]{2,1,0:T(8,128)(2,1)}, bf16[1,256,256]{2,1,0:T(8,128)(2,1)S(1)}, u32[]{:S(2)}, u32[]{:S(2)}) collective-permute-start(bf16[1,256,256]{2,1,0:T(8,128)(2,1)} %bitcast.77), channel_id=1, source_target_pairs={{0,2},{2,0},{4,6},{6,4},{8,10},{10,8},{12,14},{14,12},{1,3},{3,1},... | collective-permute-start | bytes 393224 | tf_op jit(solution)/shard_map/ppermute | solution.py:21
  15.0 7.5 %collective-permute-start.1 = (bf16[2,256,256]{2,1,0:T(8,128)(2,1)S(1)}, bf16[2,256,256]{2,1,0:T(8,128)(2,1)S(1)}, u32[]{:S(2)}, u32[]{:S(2)}) collective-permute-start(bf16[2,256,256]{2,1,0:T(8,128)(2,1)S(1)} %pad_maximum_fusion.2), channel_id=1, source_target_pairs={{0,4},{2,6},{4,0},{6,2},{8,12},{10,14},{12,8},{14,10},{1,5},{3,7},... | collective-permute-start | bytes 786440 | tf_op jit(solution)/shard_map/ppermute | solution.py:21
  23.4 27.9 %collective-permute-start.2 = (bf16[4,256,256]{2,1,0:T(8,128)(2,1)}, bf16[4,256,256]{2,1,0:T(8,128)(2,1)S(1)}, u32[]{:S(2)}, u32[]{:S(2)}) collective-permute-start(bf16[4,256,256]{2,1,0:T(8,128)(2,1)} %pad_maximum_fusion.1), channel_id=1, source_target_pairs={{0,8},{2,10},{4,12},{6,14},{8,0},{10,2},{12,4},{14,6},{1,9},{3,11}... | collective-permute-start | bytes 1572872 | tf_op jit(solution)/shard_map/ppermute | solution.py:21
Sparse Core Ops, SparseCore 0:
  12.1 51.7 all-gather.1
